TPU v7x, 128 devices: a whole 4x4x4 slice. The times are simulated.
128 devices in a mesh: dp: 4 (over x), tensor: 32 (over y, z, core).
Axes of the slice: x: 4, y: 4, z: 4, core: 2. Of those that a mesh axis runs over, the one named last changes fastest.
Arguments:
- tokens: bfloat16 [16384, 2048], P(('dp', 'tensor')), may hold values from -6 to 6
- norm_gain: bfloat16 [2048], replicated, may hold values from 0.099609375 to 1.8984375
- routes: int32 [16384, 6], P(('dp', 'tensor')), may hold values from 0 to 31, all different within a row; in each aligned block of 128 rows (0 to 127, 128 to 255, ...) at most 32 rows name the same one
- route_gates: bfloat16 [16384, 6], P(('dp', 'tensor')), may hold values from 0.19921875 to 1
- lengths: int32 [24], replicated, may hold values from 1 to 1920, 16384 in all
- request_adapter: int32 [24], replicated, may hold values from 0 to 31
- adapter_slot: int32 [32], replicated, may hold values from 0 to 31, each once
- expert_gate: bfloat16 [32, 2048, 1408], P('tensor'), may hold values from -0.125 to 0.125
- expert_up: bfloat16 [32, 2048, 1408], P('tensor'), may hold values from -0.125 to 0.125
- expert_down: bfloat16 [32, 1408, 2048], P('tensor'), may hold values from -0.15625 to 0.15625
- shared_gate: bfloat16 [2048, 1408], P(None, 'dp'), may hold values from -0.125 to 0.125
- shared_up_weight: bfloat16 [2048, 1408], P(None, 'dp'), may hold values from -0.125 to 0.125
- shared_down: bfloat16 [1408, 2048], P('dp'), may hold values from -0.15625 to 0.15625
- adapter_down: bfloat16 [32, 2048, 16], P('dp'), may hold values from -0.125 to 0.125
- adapter_up: bfloat16 [32, 16, 2048], P('dp'), may hold values from -1.5 to 1.5
- head_weight: bfloat16 [2048, 65536], P(None, ('dp', 'tensor')), may hold values from -0.375 to 0.375
Outputs:
- sublayer_out: bfloat16 [16384, 2048], P(('dp', 'tensor'))
- last_norm: float32 [24], replicated
- block_logit: float32 [24, 32], P(None, 'tensor')
Inputs may be any that keep to these rules, and one draw needn't show every extreme that they name: `routes`: in each aligned block of 128 rows (the rows of one device), no expert is named by more than 32 rows, a bound that some block reaches. The lengths sum to 16384; the largest is exactly 1920. Each position of the store appears once: adapter a is stored at position adapter_slot[a] of adapter_down and adapter_up.
All inputs are finite; a program needn't handle non-finite values.
Results may differ from a plain program's by a relative error of at most 0.0066.
Values may be sent and summed in bfloat16 or wider, within the bound.
A program may use at most 128 MiB of HBM per device.

v0:
```python
import jax
import jax.numpy as jnp
from jax import lax
from jax.sharding import PartitionSpec as P

CAP = 32


def apply_norm(tokens, norm_gain):
    values = tokens.astype(jnp.float32)
    scaled = lax.rsqrt(jnp.mean(values * values, axis=-1, keepdims=True) + 1e-06)
    return (values * scaled * norm_gain.astype(jnp.float32)).astype(jnp.bfloat16)


def feed_forward(inputs, gate_mat, up_mat, down_mat):
    gate_portion = jnp.dot(inputs, gate_mat, preferred_element_type=jnp.float32)
    up_part = jnp.dot(inputs, up_mat, preferred_element_type=jnp.float32)
    hidden = (jax.nn.silu(gate_portion) * up_part).astype(jnp.bfloat16)
    return jnp.dot(hidden, down_mat, preferred_element_type=jnp.float32)


def token_slots(positions, lengths, request_adapter, adapter_slot):
    request_ends = jnp.cumsum(lengths)
    request = jnp.sum((request_ends[None, :] <= positions[:, None]).astype(jnp.int32), axis=1)
    request_pick = (
        request[:, None] == jnp.arange(request_adapter.shape[0], dtype=jnp.int32)[None, :]
    )
    adapter = jnp.sum(jnp.where(request_pick, request_adapter[None, :], 0), axis=1)
    adapter_pick = adapter[:, None] == jnp.arange(adapter_slot.shape[0], dtype=jnp.int32)[None, :]
    return jnp.sum(jnp.where(adapter_pick, adapter_slot[None, :], 0), axis=1)


def adapter_delta(inputs, slot_ids, down_store, up_store):
    held_count = down_store.shape[0]
    model_width = down_store.shape[1]
    rank_size = down_store.shape[2]
    flat_down = jnp.transpose(down_store, (1, 0, 2)).reshape(model_width, held_count * rank_size)
    low_rank = jnp.dot(inputs, flat_down, preferred_element_type=jnp.float32)
    low_rank = low_rank.reshape(inputs.shape[0], held_count, rank_size)
    keep_mask = slot_ids[:, None] == jnp.arange(held_count, dtype=jnp.int32)[None, :]
    low_rank = jnp.where(keep_mask[:, :, None], low_rank, 0.0).astype(jnp.bfloat16)
    low_rank = low_rank.reshape(inputs.shape[0], held_count * rank_size)
    flat_up = up_store.reshape(held_count * rank_size, up_store.shape[2])
    return jnp.dot(low_rank, flat_up, preferred_element_type=jnp.float32)


def local(
    tokens,
    norm_gain,
    routes,
    route_gates,
    lengths,
    request_adapter,
    adapter_slot,
    expert_gate,
    expert_up,
    expert_down,
    shared_gate,
    shared_up_weight,
    shared_down,
    adapter_down,
    adapter_up,
    head_weight,
):
    tok_rows = tokens.shape[0]
    model_width = tokens.shape[1]
    route_count = routes.shape[1]
    tensor_size = lax.axis_size("tensor")
    tensor_pos = lax.axis_index("tensor")
    data_pos = lax.axis_index("dp")
    local_experts = expert_gate.shape[0]
    all_experts = local_experts * tensor_size
    slot_range = jnp.arange(CAP, dtype=jnp.int32)
    normed = apply_norm(tokens, norm_gain)
    numbers = jnp.arange(all_experts, dtype=jnp.int32)
    route_hits = routes[:, :, None] == numbers[None, None, :]
    chosen = jnp.any(route_hits, axis=1)
    weight = jnp.sum(
        jnp.where(route_hits, route_gates[:, :, None], jnp.zeros((), jnp.bfloat16)), axis=1
    )
    slot_place = jnp.cumsum(chosen.astype(jnp.int32), axis=0) - 1
    pooled, pooled_routes = (
        lax.all_gather(normed, "tensor", axis=0, tiled=True),
        lax.all_gather(routes.astype(jnp.bfloat16), "tensor", axis=0, tiled=True),
    )
    pooled = pooled.reshape(tensor_size, tok_rows, model_width)
    source_routes = pooled_routes.astype(jnp.int32).reshape(tensor_size, tok_rows, route_count)
    own_numbers = tensor_pos * local_experts + jnp.arange(local_experts, dtype=jnp.int32)
    source_hits = source_routes[:, :, :, None] == own_numbers[None, None, None, :]
    source_chosen = jnp.any(source_hits, axis=2)
    source_place = jnp.cumsum(source_chosen.astype(jnp.int32), axis=1) - 1
    source_pick = source_chosen[:, :, :, None] & (
        source_place[:, :, :, None] == slot_range[None, None, None, :]
    )
    source_pick = jnp.where(source_pick, 1.0, 0.0).astype(jnp.bfloat16)
    incoming = jnp.einsum(
        "sijc,sid->sjcd", source_pick, pooled, preferred_element_type=jnp.float32
    ).astype(jnp.bfloat16)
    gate_portion = jnp.einsum(
        "secd,edf->secf", incoming, expert_gate, preferred_element_type=jnp.float32
    )
    up_part = jnp.einsum("secd,edf->secf", incoming, expert_up, preferred_element_type=jnp.float32)
    hidden = (jax.nn.silu(gate_portion) * up_part).astype(jnp.bfloat16)
    expert_out = jnp.einsum(
        "secf,efd->secd", hidden, expert_down, preferred_element_type=jnp.float32
    ).astype(jnp.bfloat16)
    returned_rows = lax.all_to_all(expert_out, "tensor", split_axis=0, concat_axis=0, tiled=True)
    returned_rows = returned_rows.reshape(all_experts, CAP, model_width)
    mixing_result = jnp.where(
        slot_place[:, :, None] == slot_range[None, None, :],
        weight[:, :, None],
        jnp.zeros((), jnp.bfloat16),
    )
    routed_output = jnp.einsum(
        "kbt,btw->kw", mixing_result, returned_rows, preferred_element_type=jnp.float32
    )
    own_base = (data_pos * tensor_size + tensor_pos) * tok_rows
    own_positions = own_base + jnp.arange(tok_rows, dtype=jnp.int32)
    peer_rows = lax.all_gather(normed, "dp", axis=0, tiled=True)
    shared_sum = lax.psum_scatter(
        feed_forward(peer_rows, shared_gate, shared_up_weight, shared_down),
        "dp",
        scatter_dimension=0,
        tiled=True,
    )
    own_slots = token_slots(own_positions, lengths, request_adapter, adapter_slot)
    store_down, store_up = (
        lax.all_gather(adapter_down, "dp", axis=0, tiled=True),
        lax.all_gather(adapter_up, "dp", axis=0, tiled=True),
    )
    summed = routed_output + shared_sum + adapter_delta(normed, own_slots, store_down, store_up)
    sublayer_out = summed.astype(jnp.bfloat16)
    request_ends = jnp.cumsum(lengths)
    last_pick = jnp.where(request_ends[:, None] - 1 == own_positions[None, :], 1.0, 0.0).astype(
        jnp.bfloat16
    )
    last_part = jnp.dot(last_pick, sublayer_out, preferred_element_type=jnp.float32)
    last_states = lax.psum(last_part, ("dp", "tensor"))
    last_norm = jnp.sqrt(jnp.sum(last_states * last_states, axis=1))
    logits = jnp.dot(
        last_states.astype(jnp.bfloat16), head_weight, preferred_element_type=jnp.float32
    )
    block_logit = lax.pmax(jnp.max(logits, axis=1), "dp")
    return (sublayer_out, last_norm, block_logit[:, None])


def solution(mesh):
    placed = (
        P(("dp", "tensor"), None),
        P(),
        P(("dp", "tensor"), None),
        P(("dp", "tensor"), None),
        P(),
        P(),
        P(),
        P("tensor", None, None),
        P("tensor", None, None),
        P("tensor", None, None),
        P(None, "dp"),
        P(None, "dp"),
        P("dp", None),
        P("dp", None, None),
        P("dp", None, None),
        P(None, ("dp", "tensor")),
    )
    return jax.shard_map(
        local,
        mesh=mesh,
        in_specs=placed,
        out_specs=(P(("dp", "tensor"), None), P(), P(None, "tensor")),
        check_vma=False,
    )
```

profile of v0, /device:TPU:0, one launch (start us, length us, event | category | flops | bytes accessed | tf_op | source)
XLA Modules:
  0.0 401.9 jit_solution(9235097486257809376)
XLA Ops:
  7.2 0.0 all-gather.7.cloned.1.call-start
  7.2 0.9 convert_element_type.84
  8.1 1.3 fusion.41
  9.4 2.0 fusion.43
  11.4 0.0 all-gather.7.cloned.1.call-update
  11.5 0.0 all-gather.5.cloned.1.call-start
  11.5 0.7 all-gather.5.cloned.1.call-update
  12.2 0.0 reduce-scatter.2.cloned.1.call-start
  12.3 32.6 %all-gather.7.cloned.1.call-done = bf16[512,2048]{1,0:T(8,128)(2,1)} async-done(((bf16[128,2048]{1,0:T(8,128)(2,1)}), bf16[512,2048]{1,0:T(8,128)(2,1)}) %all-gather.7.cloned.1.call-update) | async-done | bytes 2097168 | tf_op jit(solution)/shard_map/all_gather | solution.py:119
  44.9 3.8 fusion.82
  48.7 6.3 %fusion.32 = f32[512,2048]{1,0:T(8,128)} fusion(bf16[352,2048]{1,0:T(8,128)(2,1)S(1)} %copy-done.8, bf16[512,2048]{1,0:T(8,128)(2,1)} %all-gather.7.cloned.1.call-done, bf16[2048,352]{0,1:T(8,128)(2,1)} %param.27, f32[512,352]{0,1:T(8,128)} %fusion.82), kind=kOutput, calls=%fused_computation.29 | convolution fusion | flops 1477476352 | bytes 9895936 | tf_op jit(solution)/shard_map/dot_general | solution.py:19
  55.0 0.0 reduce-scatter.2.cloned.1.call-update
  55.0 0.0 all-gather.11.cloned.1.call-start
  55.1 1.0 copy-done.4
  56.0 1.1 copy.47
  57.2 24.6 %all_gather.15 = bf16[4096,6]{0,1:T(8,128)(2,1)S(1)} all-gather(bf16[128,6]{0,1:T(8,128)(2,1)S(1)} %convert_element_type.79), channel_id=1, replica_groups=mesh['dp'=4,'tensor'=32] {'tensor'}, dimensions={0}, use_global_device_ids=true | all-gather | bytes 50688 | tf_op jit(solution)/shard_map/all_gather | solution.py:84
  81.7 0.1 fusion.63
  81.8 0.3 reduce_window_sum.31
  82.1 38.3 %all-gather.5.cloned.1.call-done = bf16[4096,2048]{1,0:T(8,128)(2,1)} async-done(((bf16[128,2048]{1,0:T(8,128)(2,1)}), bf16[4096,2048]{1,0:T(8,128)(2,1)}) %all-gather.5.cloned.1.call-update) | async-done | bytes 16777232 | tf_op jit(solution)/shard_map/all_gather | solution.py:83
  120.4 8.1 %convolution_convert_fusion = bf16[32,32,2048]{2,1,0:T(8,128)(2,1)S(1)} fusion(bf16[32,128,2048]{2,1,0:T(8,128)(2,1)} %bitcast.109, s32[32,128]{1,0:T(8,128)S(1)} %broadcast_add_fusion.1, pred[32,128]{1,0:T(8,128)(4,1)S(1)} %bitcast.111), kind=kOutput, calls=%fused_computation.16 | convolution fusion | flops 539492352 | bytes 20992000 | tf_op jit(solution)/shard_map/sijc,sid->sjcd/dot_general | solution.py:96
  128.5 2.1 copy-done.1
  130.6 10.7 %fusion.3 = f32[32,32,1408]{2,1,0:T(8,128)} fusion(bf16[32,32,2048]{2,1,0:T(8,128)(2,1)S(1)} %convolution_convert_fusion, bf16[1,2048,1408]{2,1,0:T(8,128)(2,1)} %param.24), kind=kOutput, calls=%fused_computation.4 | convolution fusion | flops 5905580032 | bytes 15728640 | tf_op jit(solution)/shard_map/secd,edf->secf/dot_general | solution.py:102
  141.3 21.0 %convert_bitcast_fusion = bf16[32,1,32,2048]{3,2,1,0:T(8,128)(2,1)} fusion(bf16[1,1408,2048]{2,1,0:T(8,128)(2,1)} %param.25, f32[32,32,1408]{2,1,0:T(8,128)} %fusion.3, bf16[32,32,2048]{2,1,0:T(8,128)(2,1)} %copy-done.1, bf16[1,2048,1408]{2,1,0:T(8,128)(2,1)} %param.23), kind=kOutput, calls=%fused_computation.15 | convolution fusion | flops 11821907968 | bytes 25690112 | tf_op jit(solution)/shard_map/secf,efd->secd/dot_general | solution.py:104
  162.4 5.2 %all-to-all-start = ((bf16[32,1,32,2048]{3,2,1,0:T(8,128)(2,1)}), bf16[32,1,32,2048]{3,2,1,0:T(8,128)(2,1)}, u32[]{:S(2)}, u32[]{:S(2)}) async-start(bf16[32,1,32,2048]{3,2,1,0:T(8,128)(2,1)} %convert_bitcast_fusion), calls=%async_computation | async-start | bytes 8388608 | tf_op jit(solution)/shard_map/all_to_all | solution.py:107
  167.6 0.0 all-gather.9.cloned.1.call-start
  167.7 0.5 all-gather.9.cloned.1.call-update
  168.2 0.3 all-reduce.2.cloned.1.call-start
  168.5 0.1 copy.42
  168.6 0.2 reduce_window_sum.30
  168.8 0.1 copy.43
  168.8 0.1 copy.45
  168.9 0.1 reduce-window.7
  169.0 0.1 reduce.2
  169.1 0.1 convert_reduce_fusion
  169.2 0.1 select_reduce_fusion.1
  169.3 0.1 select_reduce_fusion
  169.5 0.0 reduce-scatter.2.cloned.1.call-done
  169.5 50.9 %all-to-all-done = bf16[32,1,32,2048]{3,2,1,0:T(8,128)(2,1)} async-done(((bf16[32,1,32,2048]{3,2,1,0:T(8,128)(2,1)}), bf16[32,1,32,2048]{3,2,1,0:T(8,128)(2,1)}, u32[]{:S(2)}, u32[]{:S(2)}) %all-to-all-start) | async-done | bytes 4194336 | tf_op jit(solution)/shard_map/all_to_all | solution.py:107
  220.4 4.3 %fusion.23 = f32[128,2048]{1,0:T(8,128)} fusion(f32[128,2048]{1,0:T(8,128)} %reduce-scatter.2.cloned.1.call-done, bf16[32,1,32,2048]{3,2,1,0:T(8,128)(2,1)} %all-to-all-done, s32[128,32]{0,1:T(8,128)S(1)} %copy.43, bf16[128,32]{0,1:T(8,128)(2,1)S(1)} %fusion.68), kind=kOutput, calls=%fused_computation.21 | convolution fusion | flops 537395200 | bytes 6316032 | tf_op jit(solution)/shard_map/kbt,btw->kw/dot_general | solution.py:114
  224.7 9.1 %all-gather.9.cloned.1.call-done = bf16[32,2048,16]{1,2,0:T(8,128)(2,1)} async-done(((bf16[8,2048,16]{1,2,0:T(8,128)(2,1)}), bf16[32,2048,16]{1,2,0:T(8,128)(2,1)}) %all-gather.9.cloned.1.call-update) | async-done | bytes 2097168 | tf_op jit(solution)/shard_map/all_gather | solution.py:128
  233.7 4.5 %fusion.26 = bf16[128,2048]{1,0:T(8,128)(2,1)S(1)} fusion(f32[128,2048]{1,0:T(8,128)} %fusion.23, bf16[32,16,2048]{2,0,1:T(8,128)(2,1)} %all-gather.11.cloned.1.call-done, bf16[32,16,2048]{2,1,0:T(8,128)(2,1)} %bitcast.110, bf16[128,2048]{1,0:T(8,128)(2,1)S(1)} %copy-done.2, pred[128,32]{0,1:T(8,128)(4,1)S(1)} %iota_compare_fusion.3), kind=kOutput, calls=%fused_computation.22 | convolution fusion | flops 537526272 | bytes 6295552 | tf_op jit(solution)/shard_map/dot_general | solution.py:44
  238.3 0.9 fusion.69
  239.2 0.0 all-reduce.2.cloned.1.call-update
  239.2 143.1 %all-reduce.2.cloned.1.call-done = f32[24,2048]{1,0:T(8,128)} async-done(((f32[24,2048]{1,0:T(8,128)}), f32[24,2048]{1,0:T(8,128)}) %all-reduce.2.cloned.1.call-update) | async-done | bytes 196624 | tf_op jit(solution)/shard_map/psum | solution.py:138
  382.3 1.4 convolution_reduce_fusion
  383.7 9.7 %pmax.7 = f32[24,1]{0,1:T(1,128)} all-reduce(f32[24,1]{0,1:T(1,128)S(1)} %bitcast.112), channel_id=1, replica_groups=mesh['dp'=4,'tensor'=32] {'dp'}, use_global_device_ids=true, to_apply=%region_14.15 | all-reduce | flops 24 | bytes 192 | tf_op jit(solution)/shard_map/pmax | solution.py:143
  393.5 1.1 multiply_reduce_fusion
  394.6 0.5 sqrt.3
  (33 shorter events, 0.2 us)
Async XLA Ops:
  7.2 375.2 %copy-start = (bf16[2048,512]{1,0:T(8,128)(2,1)S(1)}, bf16[2048,512]{1,0:T(8,128)(2,1)}, u32[]{:S(2)}) copy-start(bf16[2048,512]{1,0:T(8,128)(2,1)} %param.31) | copy-start | bytes 6291460
  7.2 41.5 %copy-start.8 = (bf16[352,2048]{1,0:T(8,128)(2,1)S(1)}, bf16[352,2048]{1,0:T(8,128)(2,1)}, u32[]{:S(2)}) copy-start(bf16[352,2048]{1,0:T(8,128)(2,1)} %param.28) | copy-start | bytes 4325380
  7.2 37.7 %all-gather.7.cloned.1.call-start = ((), (), s32[]{:S(2)}) async-start(), calls=%async_computation.3 | async-start | bytes 2621440 | tf_op jit(solution)/shard_map/all_gather | solution.py:119
  11.5 109.0 %all-gather.5.cloned.1.call-start = ((), (), s32[]{:S(2)}) async-start(), calls=%async_computation.2 | async-start | bytes 17301504 | tf_op jit(solution)/shard_map/all_gather | solution.py:83
  12.2 157.3 %reduce-scatter.2.cloned.1.call-start = ((), (), s32[]{:S(2)}) async-start(), calls=%async_computation.4 | async-start | bytes 5242880 | tf_op jit(solution)/shard_map/reduce_scatter | solution.py:120
  55.0 1.0 copy-start.4
  55.0 2.1 copy-start.5
  55.0 169.6 %all-gather.11.cloned.1.call-start = ((), (), s32[]{:S(2)}) async-start(), calls=%async_computation.6 | async-start | bytes 2621440 | tf_op jit(solution)/shard_map/all_gather | solution.py:129
  128.5 2.1 copy-start.1
  162.3 6.5 %copy-start.7 = (s32[24]{0:T(128)S(1)}, s32[24]{0:T(128)}, u32[]{:S(2)}) copy-start(s32[24]{0:T(128)} %param.20) | copy-start | bytes 292
  162.3 6.9 %copy-start.9 = (s32[24]{0:T(128)S(1)}, s32[24]{0:T(128)}, u32[]{:S(2)}) copy-start(s32[24]{0:T(128)} %param.21) | copy-start | bytes 292
  162.3 7.0 %copy-start.10 = (s32[32]{0:T(128)S(1)}, s32[32]{0:T(128)}, u32[]{:S(2)}) copy-start(s32[32]{0:T(128)} %param.22) | copy-start | bytes 388
  162.4 7.1 %copy-start.6 = (bf16[128,6]{0,1:T(8,128)(2,1)S(1)}, bf16[128,6]{0,1:T(8,128)(2,1)}, u32[]{:S(2)}) copy-start(bf16[128,6]{0,1:T(8,128)(2,1)} %param.19) | copy-start | bytes 4612
  162.4 58.0 %all-to-all-start = ((bf16[32,1,32,2048]{3,2,1,0:T(8,128)(2,1)}), bf16[32,1,32,2048]{3,2,1,0:T(8,128)(2,1)}, u32[]{:S(2)}, u32[]{:S(2)}) async-start(bf16[32,1,32,2048]{3,2,1,0:T(8,128)(2,1)} %convert_bitcast_fusion), calls=%async_computation | async-start | bytes 8388608 | tf_op jit(solution)/shard_map/all_to_all | solution.py:107
  167.6 66.1 %copy-start.2 = (bf16[128,2048]{1,0:T(8,128)(2,1)S(1)}, bf16[128,2048]{1,0:T(8,128)(2,1)}, u32[]{:S(2)}) copy-start(bf16[128,2048]{1,0:T(8,128)(2,1)} %fusion.43) | copy-start | bytes 1572868
  167.6 66.1 %all-gather.9.cloned.1.call-start = ((), (), s32[]{:S(2)}) async-start(), calls=%async_computation.5 | async-start | bytes 2621440 | tf_op jit(solution)/shard_map/all_gather | solution.py:128
  168.2 214.1 %all-reduce.2.cloned.1.call-start = ((), (), s32[]{:S(2)}) async-start(), calls=%async_computation.7 | async-start | bytes 393216 | tf_op jit(solution)/shard_map/psum | solution.py:138
  238.3 156.8 %copy-start.3 = (bf16[128,2048]{1,0:T(8,128)(2,1)}, bf16[128,2048]{1,0:T(8,128)(2,1)S(1)}, u32[]{:S(2)}) copy-start(bf16[128,2048]{1,0:T(8,128)(2,1)S(1)} %fusion.26) | copy-start | bytes 1572868
Sparse Core Ops, SparseCore 0:
  11.6 33.2 all-gather.6
  47.7 72.6 all-gather.4
  122.8 46.1 reduce-scatter.1
  170.7 30.5 all-gather.10
  202.9 30.8 all-gather.8
  239.3 142.9 all-reduce.1
where the time goes:
time: 402 us
  waiting for transfers between devices  275 us (68%)
  matrix products  61.1 us (15%)
  blocking collectives  34.3 us (9%)
  between operations  14.3 us (4%)
  other arithmetic  6.28 us (2%)
  starting transfers between devices  5.69 us (1%)
  local copies, waits for them, and re-layouts  4.94 us (1%)
    psum x1, waiting for transfers between devices, local(): last_states = lax.psum(last_part, ('dp', 'tensor'))  143 us
    all_to_all x1, waiting for transfers between devices, local(): lax.all_to_all(expert_out, 'tensor', split_axis=0, concat_axis=0, tiled=T...  50.9 us
    all_gather x1, waiting for transfers between devices, local(): lax.all_gather(normed, 'tensor', axis=0, tiled=True)  38.3 us
    all_gather x1, waiting for transfers between devices, local(): peer_rows = lax.all_gather(normed, 'dp', axis=0, tiled=True)  32.6 us
    all_gather x1, blocking collectives, local(): lax.all_gather(routes.astype(jnp.bfloat16), 'tensor', axis=0, tiled=True)  24.6 us
    dot_general x1, matrix products, local(): jnp.einsum('secf,efd->secd', hidden, expert_down, preferred_element_type=...  21 us
    dot_general x1, matrix products, local(): jnp.einsum('secd,edf->secf', incoming, expert_up, preferred_element_type=...  10.7 us
    pmax x1, blocking collectives, local(): block_logit = lax.pmax(jnp.max(logits, axis=1), 'dp')  9.75 us
  transfers between devices with their start and end apart: 7, of which 5 were waited for; matrix products, arithmetic and copies ran while one was open for 14% of the time, Pallas kernels for 0%

commit v1 on v0

--- a/solution.py
+++ b/solution.py
@@ -135,7 +135,8 @@
         jnp.bfloat16
     )
     last_part = jnp.dot(last_pick, sublayer_out, preferred_element_type=jnp.float32)
-    last_states = lax.psum(last_part, ("dp", "tensor"))
+    terms = lax.all_gather(last_part, ("dp", "tensor"))
+    last_states = jnp.sum(terms, axis=0)
     last_norm = jnp.sqrt(jnp.sum(last_states * last_states, axis=1))
     logits = jnp.dot(
         last_states.astype(jnp.bfloat16), head_weight, preferred_element_type=jnp.float32

time: 402 us -> 361 us (0.90)
  waiting for transfers between devices: 275 us -> 227 us
  other arithmetic: 6.28 us -> 14.5 us
    psum x1 -> x0, waiting for transfers between devices: 143 us -> none  [local(): last_states = lax.psum(last_part, ('dp', 'tensor'))]
    all_gather x0 -> x1, waiting for transfers between devices: none -> 93.3 us  [local(): terms = lax.all_gather(last_part, ('dp', 'tensor'))]
    reduce_sum x0 -> x1, other arithmetic: none -> 9.17 us  [local(): last_states = jnp.sum(terms, axis=0)]
    all_gather x1, waiting for transfers between devices: 0.01 us -> 9.13 us  [local(): lax.all_gather(adapter_up, 'dp', axis=0, tiled=True)]
    all_gather x1, waiting for transfers between devices: 9.08 us -> 0.01 us  [local(): lax.all_gather(adapter_down, 'dp', axis=0, tiled=True)]
  transfers between devices with their start and end apart: 7 -> 7, of which waited for: 5 -> 5; matrix products, arithmetic and copies ran while one was open for 14% -> 16% of each run, Pallas kernels for 0% -> 0%
where the time goes in v1:
time: 361 us
  waiting for transfers between devices  227 us (63%)
  matrix products  60.2 us (17%)
  blocking collectives  35.4 us (10%)
  other arithmetic  14.5 us (4%)
  between operations  14.3 us (4%)
  starting transfers between devices  5.65 us (2%)
  local copies, waits for them, and re-layouts  4.07 us (1%)
    all_gather x1, waiting for transfers between devices, local(): terms = lax.all_gather(last_part, ('dp', 'tensor'))  93.3 us
    all_to_all x1, waiting for transfers between devices, local(): lax.all_to_all(expert_out, 'tensor', split_axis=0, concat_axis=0, tiled=T...  50.3 us
    all_gather x1, waiting for transfers between devices, local(): lax.all_gather(normed, 'tensor', axis=0, tiled=True)  40 us
    all_gather x1, waiting for transfers between devices, local(): peer_rows = lax.all_gather(normed, 'dp', axis=0, tiled=True)  32.6 us
    all_gather x1, blocking collectives, local(): lax.all_gather(routes.astype(jnp.bfloat16), 'tensor', axis=0, tiled=True)  24.5 us
    dot_general x1, matrix products, local(): jnp.einsum('secf,efd->secd', hidden, expert_down, preferred_element_type=...  21 us
    pmax x1, blocking collectives, local(): block_logit = lax.pmax(jnp.max(logits, axis=1), 'dp')  10.9 us
    dot_general x1, matrix products, local(): jnp.einsum('secd,edf->secf', incoming, expert_up, preferred_element_type=...  10.8 us
  transfers between devices with their start and end apart: 7, of which 5 were waited for; matrix products, arithmetic and copies ran while one was open for 16% of the time, Pallas kernels for 0%

profile of v1, /device:TPU:0, one launch (start us, length us, event | category | flops | bytes accessed | tf_op | source)
XLA Modules:
  0.0 360.7 jit_solution(14780994323421316763)
XLA Ops:
  7.2 0.0 all-gather.9.cloned.1.call-start
  7.2 1.4 fusion.41
  8.7 0.7 convert_element_type.84
  9.3 2.0 fusion.43
  11.4 0.0 all-gather.9.cloned.1.call-update
  11.4 0.0 all-gather.7.cloned.1.call-start
  11.4 0.7 all-gather.7.cloned.1.call-update
  12.1 0.0 reduce-scatter.2.cloned.1.call-start
  12.2 32.6 %all-gather.9.cloned.1.call-done = bf16[512,2048]{1,0:T(8,128)(2,1)} async-done(((bf16[128,2048]{1,0:T(8,128)(2,1)}), bf16[512,2048]{1,0:T(8,128)(2,1)}) %all-gather.9.cloned.1.call-update) | async-done | bytes 2097168 | tf_op jit(solution)/shard_map/all_gather | solution.py:119
  44.8 3.8 %fusion.82 = f32[512,352]{0,1:T(8,128)} fusion(bf16[512,2048]{1,0:T(8,128)(2,1)} %all-gather.9.cloned.1.call-done, bf16[2048,352]{0,1:T(8,128)(2,1)} %param.26), kind=kOutput, calls=%fused_computation.91 | convolution fusion | flops 738197504 | bytes 4259840 | tf_op jit(solution)/shard_map/dot_general | solution.py:16
  48.6 6.3 %fusion.32 = f32[512,2048]{1,0:T(8,128)} fusion(bf16[352,2048]{1,0:T(8,128)(2,1)S(1)} %copy-done.8, bf16[512,2048]{1,0:T(8,128)(2,1)} %all-gather.9.cloned.1.call-done, bf16[2048,352]{0,1:T(8,128)(2,1)} %param.27, f32[512,352]{0,1:T(8,128)} %fusion.82), kind=kOutput, calls=%fused_computation.29 | convolution fusion | flops 1477476352 | bytes 9895936 | tf_op jit(solution)/shard_map/dot_general | solution.py:19
  54.9 0.0 reduce-scatter.2.cloned.1.call-update
  55.0 0.0 all-gather.11.cloned.1.call-start
  55.0 0.5 all-gather.11.cloned.1.call-update
  55.5 0.1 copy-done.5
  55.6 24.5 %all_gather.21 = bf16[4096,6]{0,1:T(8,128)(2,1)S(1)} all-gather(bf16[128,6]{0,1:T(8,128)(2,1)S(1)} %convert_element_type.79), channel_id=1, replica_groups=mesh['dp'=4,'tensor'=32] {'tensor'}, dimensions={0}, use_global_device_ids=true | all-gather | bytes 50688 | tf_op jit(solution)/shard_map/all_gather | solution.py:84
  80.2 0.1 fusion.63
  80.2 0.3 reduce_window_sum.31
  80.5 40.0 %all-gather.7.cloned.1.call-done = bf16[4096,2048]{1,0:T(8,128)(2,1)} async-done(((bf16[128,2048]{1,0:T(8,128)(2,1)}), bf16[4096,2048]{1,0:T(8,128)(2,1)}) %all-gather.7.cloned.1.call-update) | async-done | bytes 16777232 | tf_op jit(solution)/shard_map/all_gather | solution.py:83
  120.5 8.1 %convolution_convert_fusion = bf16[32,32,2048]{2,1,0:T(8,128)(2,1)S(1)} fusion(bf16[32,128,2048]{2,1,0:T(8,128)(2,1)} %bitcast.110, s32[32,128]{1,0:T(8,128)S(1)} %broadcast_add_fusion.1, pred[32,128]{1,0:T(8,128)(4,1)S(1)} %bitcast.113), kind=kOutput, calls=%fused_computation.16 | convolution fusion | flops 539492352 | bytes 20992000 | tf_op jit(solution)/shard_map/sijc,sid->sjcd/dot_general | solution.py:96
  128.6 2.1 copy-done.1
  130.7 10.8 %fusion.3 = f32[32,32,1408]{2,1,0:T(8,128)} fusion(bf16[32,32,2048]{2,1,0:T(8,128)(2,1)S(1)} %convolution_convert_fusion, bf16[1,2048,1408]{2,1,0:T(8,128)(2,1)} %param.24), kind=kOutput, calls=%fused_computation.4 | convolution fusion | flops 5905580032 | bytes 15728640 | tf_op jit(solution)/shard_map/secd,edf->secf/dot_general | solution.py:102
  141.4 21.0 %convert_bitcast_fusion = bf16[32,1,32,2048]{3,2,1,0:T(8,128)(2,1)} fusion(bf16[1,1408,2048]{2,1,0:T(8,128)(2,1)} %param.25, f32[32,32,1408]{2,1,0:T(8,128)} %fusion.3, bf16[32,32,2048]{2,1,0:T(8,128)(2,1)} %copy-done.1, bf16[1,2048,1408]{2,1,0:T(8,128)(2,1)} %param.23), kind=kOutput, calls=%fused_computation.15 | convolution fusion | flops 11821907968 | bytes 25690112 | tf_op jit(solution)/shard_map/secf,efd->secd/dot_general | solution.py:104
  162.5 5.2 %all-to-all-start = ((bf16[32,1,32,2048]{3,2,1,0:T(8,128)(2,1)}), bf16[32,1,32,2048]{3,2,1,0:T(8,128)(2,1)}, u32[]{:S(2)}, u32[]{:S(2)}) async-start(bf16[32,1,32,2048]{3,2,1,0:T(8,128)(2,1)} %convert_bitcast_fusion), calls=%async_computation | async-start | bytes 8388608 | tf_op jit(solution)/shard_map/all_to_all | solution.py:107
  167.7 0.0 all-gather.13.cloned.1.call-start
  167.7 1.1 copy.47
  168.9 0.3 all-gather.15.cloned.1.call-start
  169.2 0.1 copy.45
  169.3 0.1 reduce.2
  169.4 0.1 copy.42
  169.5 0.2 reduce_window_sum.30
  169.7 0.1 copy.43
  169.8 0.1 convert_reduce_fusion
  169.9 0.1 select_reduce_fusion.1
  170.0 0.1 select_reduce_fusion
  170.1 0.0 reduce-scatter.2.cloned.1.call-done
  170.2 50.3 %all-to-all-done = bf16[32,1,32,2048]{3,2,1,0:T(8,128)(2,1)} async-done(((bf16[32,1,32,2048]{3,2,1,0:T(8,128)(2,1)}), bf16[32,1,32,2048]{3,2,1,0:T(8,128)(2,1)}, u32[]{:S(2)}, u32[]{:S(2)}) %all-to-all-start) | async-done | bytes 4194336 | tf_op jit(solution)/shard_map/all_to_all | solution.py:107
  220.5 4.3 %fusion.23 = f32[128,2048]{1,0:T(8,128)} fusion(f32[128,2048]{1,0:T(8,128)} %reduce-scatter.2.cloned.1.call-done, bf16[32,1,32,2048]{3,2,1,0:T(8,128)(2,1)} %all-to-all-done, s32[128,32]{0,1:T(8,128)S(1)} %copy.43, bf16[128,32]{0,1:T(8,128)(2,1)S(1)} %fusion.68), kind=kOutput, calls=%fused_computation.21 | convolution fusion | flops 537395200 | bytes 6316032 | tf_op jit(solution)/shard_map/kbt,btw->kw/dot_general | solution.py:114
  224.7 9.1 %all-gather.13.cloned.1.call-done = bf16[32,16,2048]{2,0,1:T(8,128)(2,1)} async-done(((bf16[8,16,2048]{2,0,1:T(8,128)(2,1)}), bf16[32,16,2048]{2,0,1:T(8,128)(2,1)}) %all-gather.13.cloned.1.call-update) | async-done | bytes 2097168 | tf_op jit(solution)/shard_map/all_gather | solution.py:129
  233.9 4.5 %fusion.26 = bf16[128,2048]{1,0:T(8,128)(2,1)S(1)} fusion(f32[128,2048]{1,0:T(8,128)} %fusion.23, bf16[32,16,2048]{2,0,1:T(8,128)(2,1)} %all-gather.13.cloned.1.call-done, bf16[32,16,2048]{2,1,0:T(8,128)(2,1)} %bitcast.112, bf16[128,2048]{1,0:T(8,128)(2,1)S(1)} %copy-done.2, pred[128,32]{0,1:T(8,128)(4,1)S(1)} %iota_compare_fusion.3), kind=kOutput, calls=%fused_computation.22 | convolution fusion | flops 537526272 | bytes 6295552 | tf_op jit(solution)/shard_map/dot_general | solution.py:44
  238.4 0.9 fusion.69
  239.3 0.0 all-gather.15.cloned.1.call-update
  239.3 93.3 %all-gather.15.cloned.1.call-done = f32[3072,2048]{1,0:T(8,128)} async-done(((f32[24,2048]{1,0:T(8,128)}), f32[3072,2048]{1,0:T(8,128)}) %all-gather.15.cloned.1.call-update) | async-done | bytes 25165840 | tf_op jit(solution)/shard_map/all_gather | solution.py:138
  332.6 9.2 %reduce_sum.71 = f32[24,2048]{1,0:T(8,128)S(1)} reduce(f32[128,24,2048]{2,1,0:T(8,128)} %bitcast.111, f32[]{:T(128)} %constant.44.clone.1), dimensions={0}, to_apply=%region_11.12 | reduce | flops 6242304 | bytes 25362436 | tf_op jit(solution)/shard_map/reduce_sum | solution.py:139
  341.8 0.1 multiply_reduce_fusion
  341.9 0.5 convolution_reduce_fusion
  342.4 0.5 sqrt.3
  342.9 10.9 %pmax.7 = f32[24,1]{0,1:T(1,128)} all-reduce(f32[24,1]{0,1:T(1,128)S(1)} %bitcast.114), channel_id=1, replica_groups=mesh['dp'=4,'tensor'=32] {'dp'}, use_global_device_ids=true, to_apply=%region_14.15 | all-reduce | flops 24 | bytes 192 | tf_op jit(solution)/shard_map/pmax | solution.py:144
  (34 shorter events, 0.2 us)
Async XLA Ops:
  7.2 334.7 %copy-start = (bf16[2048,512]{1,0:T(8,128)(2,1)S(1)}, bf16[2048,512]{1,0:T(8,128)(2,1)}, u32[]{:S(2)}) copy-start(bf16[2048,512]{1,0:T(8,128)(2,1)} %param.31) | copy-start | bytes 6291460
  7.2 41.4 %copy-start.8 = (bf16[352,2048]{1,0:T(8,128)(2,1)S(1)}, bf16[352,2048]{1,0:T(8,128)(2,1)}, u32[]{:S(2)}) copy-start(bf16[352,2048]{1,0:T(8,128)(2,1)} %param.28) | copy-start | bytes 4325380
  7.2 37.6 %all-gather.9.cloned.1.call-start = ((), (), s32[]{:S(2)}) async-start(), calls=%async_computation.3 | async-start | bytes 2621440 | tf_op jit(solution)/shard_map/all_gather | solution.py:119
  11.4 109.1 %all-gather.7.cloned.1.call-start = ((), (), s32[]{:S(2)}) async-start(), calls=%async_computation.2 | async-start | bytes 17301504 | tf_op jit(solution)/shard_map/all_gather | solution.py:83
  12.1 158.0 %reduce-scatter.2.cloned.1.call-start = ((), (), s32[]{:S(2)}) async-start(), calls=%async_computation.4 | async-start | bytes 5242880 | tf_op jit(solution)/shard_map/reduce_scatter | solution.py:120
  54.9 0.7 copy-start.5
  55.0 169.8 %all-gather.11.cloned.1.call-start = ((), (), s32[]{:S(2)}) async-start(), calls=%async_computation.5 | async-start | bytes 2621440 | tf_op jit(solution)/shard_map/all_gather | solution.py:128
  128.6 2.1 copy-start.1
  162.4 5.3 %copy-start.4 = (bf16[8,16,2048]{2,1,0:T(8,128)(2,1)S(1)}, bf16[8,16,2048]{2,1,0:T(8,128)(2,1)}, u32[]{:S(2)}) copy-start(bf16[8,16,2048]{2,1,0:T(8,128)(2,1)} %param.30) | copy-start | bytes 1572868
  162.4 6.7 %copy-start.7 = (s32[24]{0:T(128)S(1)}, s32[24]{0:T(128)}, u32[]{:S(2)}) copy-start(s32[24]{0:T(128)} %param.20) | copy-start | bytes 292
  162.4 7.4 %copy-start.9 = (s32[24]{0:T(128)S(1)}, s32[24]{0:T(128)}, u32[]{:S(2)}) copy-start(s32[24]{0:T(128)} %param.21) | copy-start | bytes 292
  162.5 7.5 %copy-start.10 = (s32[32]{0:T(128)S(1)}, s32[32]{0:T(128)}, u32[]{:S(2)}) copy-start(s32[32]{0:T(128)} %param.22) | copy-start | bytes 388
  162.5 7.6 %copy-start.6 = (bf16[128,6]{0,1:T(8,128)(2,1)S(1)}, bf16[128,6]{0,1:T(8,128)(2,1)}, u32[]{:S(2)}) copy-start(bf16[128,6]{0,1:T(8,128)(2,1)} %param.19) | copy-start | bytes 4612
  162.5 58.0 %all-to-all-start = ((bf16[32,1,32,2048]{3,2,1,0:T(8,128)(2,1)}), bf16[32,1,32,2048]{3,2,1,0:T(8,128)(2,1)}, u32[]{:S(2)}, u32[]{:S(2)}) async-start(bf16[32,1,32,2048]{3,2,1,0:T(8,128)(2,1)} %convert_bitcast_fusion), calls=%async_computation | async-start | bytes 8388608 | tf_op jit(solution)/shard_map/all_to_all | solution.py:107
  167.7 66.2 %copy-start.2 = (bf16[128,2048]{1,0:T(8,128)(2,1)S(1)}, bf16[128,2048]{1,0:T(8,128)(2,1)}, u32[]{:S(2)}) copy-start(bf16[128,2048]{1,0:T(8,128)(2,1)} %fusion.43) | copy-start | bytes 1572868
  167.7 66.2 %all-gather.13.cloned.1.call-start = ((), (), s32[]{:S(2)}) async-start(), calls=%async_computation.6 | async-start | bytes 2621440 | tf_op jit(solution)/shard_map/all_gather | solution.py:129
  168.9 163.7 %all-gather.15.cloned.1.call-start = ((), (), s32[]{:S(2)}) async-start(), calls=%async_computation.7 | async-start | bytes 25362432 | tf_op jit(solution)/shard_map/all_gather | solution.py:138
  238.4 103.4 %copy-start.3 = (bf16[128,2048]{1,0:T(8,128)(2,1)}, bf16[128,2048]{1,0:T(8,128)(2,1)S(1)}, u32[]{:S(2)}) copy-start(bf16[128,2048]{1,0:T(8,128)(2,1)S(1)} %fusion.26) | copy-start | bytes 1572868
Sparse Core Ops, SparseCore 0:
  11.5 33.2 all-gather.8
  47.7 72.7 all-gather.6
  122.9 46.2 reduce-scatter.1
  170.8 30.5 all-gather.10
  203.0 30.8 all-gather.12
  239.5 93.0 all-gather.14
